TPU v7x, 128 devices: a whole 4x4x4 slice. The times are simulated.
128 devices in a mesh: lat: 16 (over x, y), var: 8 (over z, core).
Axes of the slice: x: 4, y: 4, z: 4, core: 2. Of those that a mesh axis runs over, the one named last changes fastest.
Arguments:
- patches: bfloat16 [96, 192, 1024], P('lat', 'var'), may hold values from -6 to 6
- norm_gain: float32 [1024], replicated, may hold values from 0.25 to 1.75
- input_proj: bfloat16 [1024, 3072], replicated, may hold values from -7 to 7
- output_proj: bfloat16 [1024, 1024], replicated, may hold values from -0.1875 to 0.1875
- level_scale: float32 [40, 1024], P('var'), may hold values from 0.1 to 1.9
- level_shift: float32 [40, 1024], P('var'), may hold values from -3 to 3
- head_weight: bfloat16 [40, 1024, 320], P('var', 'lat'), may hold values from -0.1875 to 0.1875
- targets: bfloat16 [40, 96, 192, 320], P('var', 'lat'), may hold values from -6 to 6
- level_counts: int32 [4], replicated, may hold values from 13 to 37
- tile_dataset: int32 [16, 8], P('lat'), may hold values from 0 to 3
- slot_level: int32 [40], P('var'), may hold values from 0 to 39, as said below
Outputs:
- latent: bfloat16 [96, 192, 1024], P('lat', 'var')
- grad_latent: bfloat16 [96, 192, 1024], P('lat', 'var')
- grad_head: float32 [40, 1024, 320], P('var', 'lat')
Inputs may be any that keep to these rules, and one draw needn't show every extreme that they name: `slot_level`: for each j, slots j * 5 to (j + 1) * 5 - 1 hold the levels j * 5 to (j + 1) * 5 - 1 in some order.
All inputs are finite; a program needn't handle non-finite values.
Results may differ from a plain program's by a relative error of at most 0.012.
Values may be sent and summed in bfloat16 or wider, within the bound.
A program may use at most 128 MiB of HBM per device.

v0:
```python
import math
import jax
import jax.numpy as jnp
from jax import lax
from jax.sharding import PartitionSpec as P

HEADS = 16
WH = 6
WW = 12
EPS = 1e-05


def padded(array, sides, width, wrap):
    for axis, dim in sides:
        size, length = (lax.axis_size(axis), array.shape[dim])
        up = [(i, (i + 1) % size) for i in range(size if wrap else size - 1)]
        down = [(j, i) for i, j in up]
        last = lax.slice_in_dim(array, length - width, length, axis=dim)
        initial = lax.slice_in_dim(array, 0, width, axis=dim)
        before = lax.ppermute(last, axis, up)
        after = lax.ppermute(initial, axis, down)
        array = jnp.concatenate([before, array, after], axis=dim)
    return array


def layer_norm(values, gain):
    wide = values.astype(jnp.float32)
    average = jnp.mean(wide, axis=-1, keepdims=True)
    centred = wide - average
    variance = jnp.mean(centred * centred, axis=-1, keepdims=True)
    return (centred * lax.rsqrt(variance + EPS) * gain).astype(jnp.bfloat16)


def window_attention(query_ext, keyval, row_valid, heads):
    ext_rows, ext_cols, width = query_ext.shape
    head_size = width // heads
    win_rows = ext_rows // WH
    win_cols = ext_cols // WW

    def split(values, parts):
        shaped = values.reshape(win_rows, WH, win_cols, WW, parts, heads, head_size)
        return shaped.transpose(0, 2, 1, 3, 4, 5, 6).reshape(
            win_rows * win_cols, WH * WW, parts, heads, head_size
        )

    query_win = split(query_ext, 1)[:, :, 0]
    pairs = split(keyval, 2)
    key_win = pairs[:, :, 0]
    value_win = pairs[:, :, 1]
    key_mask = jnp.broadcast_to(
        row_valid.reshape(win_rows, 1, WH, 1), (win_rows, win_cols, WH, WW)
    ).reshape(win_rows * win_cols, WH * WW)
    scores = jnp.einsum(
        "wqhd,wkhd->whqk", query_win, key_win, preferred_element_type=jnp.float32
    ) / math.sqrt(head_size)
    scores = jnp.where(key_mask[:, None, None, :], scores, -jnp.inf)
    peak = jnp.max(scores, axis=-1, keepdims=True)
    weights = jnp.exp(scores - peak)
    probs = (weights / jnp.sum(weights, axis=-1, keepdims=True)).astype(jnp.bfloat16)
    mixed = jnp.einsum("whqk,wkhd->wqhd", probs, value_win, preferred_element_type=jnp.float32)
    return (
        mixed.reshape(win_rows, win_cols, WH, WW, width)
        .transpose(0, 2, 1, 3, 4)
        .reshape(ext_rows, ext_cols, width)
    )


def slot_terms(piece, target_rows, live_cols, level_scale, level_shift, heads_full):
    piece_wide = piece.astype(jnp.float32)
    rows = (
        piece_wide[None] * level_scale[:, None, None, :] + level_shift[:, None, None, :]
    ).astype(jnp.bfloat16)
    predicted = jnp.einsum("krnd,kdo->krno", rows, heads_full, preferred_element_type=jnp.float32)
    errors = ((predicted - target_rows.astype(jnp.float32)) * live_cols[:, None, :, None]).astype(
        jnp.bfloat16
    )
    back_grad = jnp.einsum("krno,kdo->krnd", errors, heads_full, preferred_element_type=jnp.float32)
    piece_grad = jnp.sum(back_grad * level_scale[:, None, None, :], axis=0)
    head_add = jnp.einsum("krnd,krno->dko", rows, errors, preferred_element_type=jnp.float32)
    return (piece_grad, head_add)


def local(
    patches,
    norm_gain,
    input_proj,
    output_proj,
    level_scale,
    level_shift,
    head_weight,
    targets,
    level_counts,
    tile_dataset,
    slot_level,
):
    band_rows, band_cols, width = patches.shape
    half_rows = WH // 2
    half_cols = WW // 2
    lat_count = lax.axis_size("lat")
    var_count = lax.axis_size("var")
    lat_place = lax.axis_index("lat")
    ext_rows = band_rows + WH
    ext_cols = band_cols + WW
    extended = padded(patches, (("lat", 0),), half_rows, False)
    extended = padded(extended, (("var", 1),), half_cols, True)
    normed_ext = layer_norm(extended, norm_gain)
    keyval = jnp.dot(
        normed_ext.reshape(-1, width), input_proj[:, width:], preferred_element_type=jnp.float32
    )
    keyval = keyval.astype(jnp.bfloat16).reshape(ext_rows, ext_cols, 2 * width)
    normed = normed_ext[half_rows : half_rows + band_rows, half_cols : half_cols + band_cols]
    queries = jnp.dot(
        normed.reshape(-1, width), input_proj[:, :width], preferred_element_type=jnp.float32
    )
    queries = queries.astype(jnp.bfloat16).reshape(band_rows, band_cols, width)
    query_ext = jnp.pad(queries, ((half_rows, WH - half_rows), (half_cols, WW - half_cols), (0, 0)))
    global_row = lat_place * band_rows - half_rows + jnp.arange(ext_rows, dtype=jnp.int32)
    row_valid = (global_row >= 0) & (global_row < lat_count * band_rows)
    mixed = window_attention(query_ext, keyval, row_valid, HEADS)
    attn = mixed[half_rows : half_rows + band_rows, half_cols : half_cols + band_cols].astype(
        jnp.bfloat16
    )
    update = jnp.dot(
        attn.reshape(-1, width), output_proj, preferred_element_type=jnp.float32
    ).reshape(band_rows, band_cols, width)
    latent = (patches.astype(jnp.float32) + update).astype(jnp.bfloat16)
    dataset_row = tile_dataset[0]
    dataset_ids = jnp.arange(level_counts.shape[0], dtype=jnp.int32)
    tile_levels = jnp.sum(
        jnp.where(dataset_row[:, None] == dataset_ids[None, :], level_counts[None, :], 0), axis=1
    )
    live_tiles = (slot_level[None, :] < tile_levels[:, None]).astype(jnp.float32)
    heads_full = lax.all_gather(head_weight, "lat", axis=1, tiled=True)
    tile_ids = jnp.arange(var_count, dtype=jnp.int32)
    piece = lax.all_gather(latent, "var", axis=1, tiled=True)
    piece_cols = piece.shape[1]
    column_tile = jnp.arange(piece_cols, dtype=jnp.int32) // band_cols
    onehot = (column_tile[:, None] == tile_ids[None, :]).astype(jnp.float32)
    column_live = jnp.dot(onehot, live_tiles)
    piece_grad, head_add = slot_terms(
        piece, targets, column_live.T, level_scale, level_shift, heads_full
    )
    latent_terms = piece_grad
    latent_terms, head_terms = (latent_terms, head_add)
    grad_latent = lax.psum_scatter(
        latent_terms.astype(jnp.bfloat16), "var", scatter_dimension=1, tiled=True
    )
    head_terms = head_terms * (1.0 / math.sqrt(lat_count * band_rows * var_count * band_cols))
    share_rows = width // lat_count
    mine = lax.psum_scatter(
        head_terms.astype(jnp.bfloat16), "lat", scatter_dimension=0, tiled=True
    ).astype(jnp.float32)
    grad_head = jnp.transpose(mine, (1, 0, 2))
    return (latent, grad_latent, grad_head)


def solution(mesh):
    in_specs = (
        P("lat", "var", None),
        P(),
        P(),
        P(),
        P("var", None),
        P("var", None),
        P("var", "lat", None),
        P("var", "lat", None, None),
        P(),
        P("lat", None),
        P("var"),
    )
    out_specs = (P("lat", "var", None), P("lat", "var", None), P("var", "lat", None))
    return jax.shard_map(local, mesh=mesh, in_specs=in_specs, out_specs=out_specs, check_vma=False)
```

profile of v0, /device:TPU:0, one launch (start us, length us, event | category | flops | bytes accessed | tf_op | source)
XLA Modules:
  0.0 313.8 jit_solution(12802649083848093492)
XLA Ops:
  7.2 0.0 copy-start
  7.2 0.0 all-gather.3.cloned.1.call-start
  7.2 1.1 fusion.61
  8.4 3.6 %collective-permute-start = (bf16[3,24,1024]{2,1,0:T(8,128)(2,1)S(1)}, bf16[3,24,1024]{2,1,0:T(8,128)(2,1)S(1)}, u32[]{:S(2)}, u32[]{:S(2)}) collective-permute-start(bf16[3,24,1024]{2,1,0:T(8,128)(2,1)S(1)} %get-tuple-element.25), channel_id=1, source_target_pairs={{0,8},{8,16},{16,24},{24,32},{32,40},{40,48},{48,56},{56,64},{64,7... | collective-permute-start | bytes 442376 | tf_op jit(solution)/shard_map/ppermute | solution.py:20
  12.0 1.3 collective-permute-start.1
  13.3 1.8 collective-permute-done
  15.0 1.0 constant_dynamic-update-slice_fusion.1
  16.0 3.1 collective-permute-done.1
  19.2 0.1 fusion.60
  19.2 0.0 collective-permute-start.2
  19.3 2.9 collective-permute-start.3
  22.2 0.1 broadcast_in_dim.28
  22.3 0.1 broadcast_in_dim.29
  22.4 3.2 %collective-permute-done.2 = bf16[12,6,1024]{2,1,0:T(8,128)(2,1)S(1)} collective-permute-done((bf16[12,6,1024]{2,1,0:T(8,128)(2,1)S(1)}, bf16[12,6,1024]{2,1,0:T(8,128)(2,1)S(1)}, u32[]{:S(2)}, u32[]{:S(2)}) %collective-permute-start.2) | collective-permute-done | bytes 147488 | tf_op jit(solution)/shard_map/ppermute | solution.py:20
  25.6 0.4 fusion.58
  26.0 0.1 div.33
  26.1 1.8 multiply_reduce_fusion.1
  27.9 0.1 rsqrt.13
  28.0 0.1 slice.45
  28.1 1.6 maximum_convert_fusion
  29.7 2.7 reshape.102
  32.4 1.3 fusion.50
  33.7 2.1 fusion.40
  35.8 0.2 pad.4
  35.9 2.1 reshape.99
  38.0 3.2 %copy.48 = bf16[2,3,6,12,1,16,64]{6,5,3,2,1,0,4:T(8,128)(2,1)} copy(bf16[2,3,6,12,1,16,64]{6,5,3,1,2,0,4:T(8,128)(2,1)} %bitcast.58) | data formatting | bytes 1769472 | tf_op jit(solution)/shard_map/transpose | solution.py:42
  41.2 5.5 %fusion.15 = bf16[432,2048]{1,0:T(8,128)(2,1)} fusion(bf16[1024,3072]{1,0:T(8,128)(2,1)} %param.13, f32[432,1024]{1,0:T(8,128)S(1)} %copy-done.2, f32[1024]{0:T(1024)S(1)} %copy-done.4, f32[432]{0:T(512)S(1)} %rsqrt.13, f32[432]{0:T(512)S(1)} %div.33), kind=kOutput, calls=%fused_computation.22 | convolution fusion | flops 1814593536 | bytes 7740800 | tf_op jit(solution)/shard_map/dot_general | solution.py:107
  46.8 6.4 %reshape_reshape.3 = bf16[2,6,3,12,2,16,64]{6,5,4,3,2,1,0:T(8,128)(2,1)} reshape(bf16[432,2048]{1,0:T(8,128)(2,1)} %fusion.15) | data formatting | bytes 3538944 | tf_op jit(solution)/shard_map/reshape;reshape | solution.py:41
  53.1 2.6 copy.46
  55.7 2.6 fusion.59
  58.3 4.0 %copy.61 = bf16[6,72,1,16,64]{1,4,3,0,2:T(8,128)(2,1)} copy(bf16[6,72,1,16,64]{4,3,2,1,0:T(8,128)(2,1)} %get-tuple-element.18) | data formatting | bytes 1769472
  62.4 4.0 %copy.62 = bf16[6,72,1,16,64]{1,4,3,0,2:T(8,128)(2,1)} copy(bf16[6,72,1,16,64]{4,3,2,1,0:T(8,128)(2,1)} %get-tuple-element.19) | data formatting | bytes 1769472
  66.4 3.1 fusion.25
  69.5 1.8 fusion.62
  71.3 1.9 fusion.34
  73.2 4.0 %copy.52 = bf16[6,72,16,64]{3,2,1,0:T(8,128)(2,1)} copy(bf16[6,72,16,64]{1,3,2,0:T(8,128)(2,1)} %fusion.34) | data formatting | bytes 1769472 | tf_op jit(solution)/shard_map/whqk,wkhd->wqhd/transpose | solution.py:60
  77.2 3.9 %reshape.100 = bf16[2,3,6,12,1024]{4,3,2,1,0:T(8,128)(2,1)} reshape(bf16[6,72,16,64]{3,2,1,0:T(8,128)(2,1)} %copy.52) | data formatting | bytes 1769472 | tf_op jit(solution)/shard_map/reshape | solution.py:62
  81.1 1.4 copy.53
  82.5 0.0 copy-start.9
  82.5 1.0 reshape.101
  83.6 2.3 fusion.43
  85.9 0.0 all-gather.3.cloned.1.call-update
  85.9 0.0 all-gather.5.cloned.1.call-start
  85.9 0.7 all-gather.5.cloned.1.call-update
  86.6 0.0 reduce-scatter.7.cloned.1.call-start
  86.7 0.1 select_reduce_fusion
  86.8 0.2 fusion.52
  87.1 28.5 %all-gather.3.cloned.1.call-done = bf16[6,192,1024]{2,1,0:T(8,128)(2,1)} async-done(((bf16[6,24,1024]{2,1,0:T(8,128)(2,1)}), bf16[6,192,1024]{2,1,0:T(8,128)(2,1)}) %all-gather.3.cloned.1.call-update) | async-done | bytes 2359312 | tf_op jit(solution)/shard_map/all_gather | solution.py:135
  115.6 4.3 %convert_element_type.67 = f32[6,192,1024]{2,1,0:T(8,128)} convert(bf16[6,192,1024]{2,1,0:T(8,128)(2,1)} %all-gather.3.cloned.1.call-done) | non-fusion elementwise | flops 1179648 | bytes 7077888 | tf_op jit(solution)/shard_map/convert_element_type | solution.py:69
  119.9 48.6 %all-gather.5.cloned.1.call-done = bf16[5,1024,320]{2,1,0:T(8,128)(2,1)} async-done(((bf16[5,64,320]{2,1,0:T(8,128)(2,1)}), bf16[5,1024,320]{2,1,0:T(8,128)(2,1)}) %all-gather.5.cloned.1.call-update) | async-done | bytes 3276816 | tf_op jit(solution)/shard_map/all_gather | solution.py:133
  168.5 10.6 %multiply_convert_fusion = bf16[5,6,192,320]{3,2,1,0:T(8,128)(2,1)S(1)} fusion(bf16[5,6,192,320]{3,2,1,0:T(8,128)(2,1)} %param.18, f32[5,192]{1,0:T(8,128)S(1)} %fusion.52, bf16[5,1024,320]{2,1,0:T(8,128)(2,1)} %all-gather.5.cloned.1.call-done, f32[5,1024]{1,0:T(8,128)S(1)} %copy-done.7, f32[5,1024]{1,0:T(8,128)S(1)} %copy-done.6, ...), kind=kOutput, calls=%fused_computation.11 | convolution fusion | flops 3799941120 | bytes 15412992 | tf_op jit(solution)/shard_map/krnd,kdo->krno/dot_general | solution.py:73
  179.2 7.2 %multiply_reduce_fusion = bf16[6,192,1024]{2,1,0:T(8,128)(2,1)S(1)} fusion(f32[5,1024]{1,0:T(8,128)S(1)} %copy-done.6, bf16[5,6,192,320]{3,2,1,0:T(8,128)(2,1)S(1)} %multiply_convert_fusion, bf16[5,1024,320]{2,1,0:T(8,128)(2,1)S(1)} %copy-done.5), kind=kOutput, calls=%fused_computation.1 | convolution fusion | flops 3785490432 | bytes 9342976 | tf_op jit(solution)/shard_map/krno,kdo->krnd/dot_general | solution.py:77
  186.4 1.7 copy.63
  188.1 0.0 reduce-scatter.7.cloned.1.call-update
  188.1 0.0 reduce-scatter.5.cloned.1.call-start
  188.2 9.3 %fusion.14 = bf16[1024,5,320]{0,2,1:T(8,128)(2,1)} fusion(bf16[5,6,192,320]{3,2,1,0:T(8,128)(2,1)} %copy-done.11, f32[5,1024]{1,0:T(8,128)S(1)} %copy-done.7, f32[5,1024]{1,0:T(8,128)S(1)} %copy-done.6, f32[6,192,1024]{2,1,0:T(8,128)} %convert_element_type.67), kind=kOutput, calls=%fused_computation.21 | convolution fusion | flops 3795845120 | bytes 11722752 | tf_op jit(solution)/shard_map/krnd,krno->dko/dot_general | solution.py:79
  197.5 8.2 %copy.54 = bf16[1024,5,320]{2,1,0:T(8,128)(2,1)} copy(bf16[1024,5,320]{0,2,1:T(8,128)(2,1)} %fusion.14) | data formatting | bytes 6553600 | tf_op jit(solution)/shard_map/convert_element_type | solution.py:151
  205.7 0.0 reduce-scatter.5.cloned.1.call-update
  205.7 16.5 %reduce-scatter.7.cloned.1.call-done = bf16[24,6144]{1,0:T(8,128)(2,1)} async-done(((bf16[192,6144]{1,0:T(8,128)(2,1)}), bf16[24,6144]{1,0:T(8,128)(2,1)}) %reduce-scatter.7.cloned.1.call-update) | async-done | bytes 294928
  222.2 1.3 reshape.107
  223.5 0.9 copy.60
  224.4 80.9 %reduce-scatter.5.cloned.1.call-done = bf16[64,5,320]{2,1,0:T(8,128)(2,1)} async-done(((bf16[1024,5,320]{2,1,0:T(8,128)(2,1)}), bf16[64,5,320]{2,1,0:T(8,128)(2,1)}) %reduce-scatter.5.cloned.1.call-update) | async-done | bytes 204816 | tf_op jit(solution)/shard_map/reduce_scatter | solution.py:150
  305.3 1.0 convert_bitcast_fusion
  306.4 0.9 copy.55
  (29 shorter events, 0.1 us)
Async XLA Ops:
  7.2 76.4 %copy-start = (bf16[1024,1024]{1,0:T(8,128)(2,1)S(1)}, bf16[1024,1024]{1,0:T(8,128)(2,1)}, u32[]{:S(2)}) copy-start(bf16[1024,1024]{1,0:T(8,128)(2,1)} %param.14) | copy-start | bytes 6291460
  7.2 108.4 %all-gather.3.cloned.1.call-start = ((), (), s32[]{:S(2)}) async-start(), calls=%async_computation.2 | async-start | bytes 2654208 | tf_op jit(solution)/shard_map/all_gather | solution.py:135
  8.4 6.7 %collective-permute-start = (bf16[3,24,1024]{2,1,0:T(8,128)(2,1)S(1)}, bf16[3,24,1024]{2,1,0:T(8,128)(2,1)S(1)}, u32[]{:S(2)}, u32[]{:S(2)}) collective-permute-start(bf16[3,24,1024]{2,1,0:T(8,128)(2,1)S(1)} %get-tuple-element.25), channel_id=1, source_target_pairs={{0,8},{8,16},{16,24},{24,32},{32,40},{40,48},{48,56},{56,64},{64,7... | collective-permute-start | bytes 442376 | tf_op jit(solution)/shard_map/ppermute | solution.py:20
  12.0 7.2 %collective-permute-start.1 = (bf16[3,24,1024]{2,1,0:T(8,128)(2,1)S(1)}, bf16[3,24,1024]{2,1,0:T(8,128)(2,1)S(1)}, u32[]{:S(2)}, u32[]{:S(2)}) collective-permute-start(bf16[3,24,1024]{2,1,0:T(8,128)(2,1)S(1)} %get-tuple-element.24), channel_id=1, source_target_pairs={{8,0},{16,8},{24,16},{32,24},{40,32},{48,40},{56,48},{64,56},{72,6... | collective-permute-start | bytes 442376 | tf_op jit(solution)/shard_map/ppermute | solution.py:21
  19.2 6.3 %collective-permute-start.2 = (bf16[12,6,1024]{2,1,0:T(8,128)(2,1)S(1)}, bf16[12,6,1024]{2,1,0:T(8,128)(2,1)S(1)}, u32[]{:S(2)}, u32[]{:S(2)}) collective-permute-start(bf16[12,6,1024]{2,1,0:T(8,128)(2,1)S(1)} %get-tuple-element.22), channel_id=1, source_target_pairs={{0,1},{1,2},{2,3},{3,4},{4,5},{5,6},{6,7},{7,0},{8,9},{9,10},{10,1... | collective-permute-start | bytes 442376 | tf_op jit(solution)/shard_map/ppermute | solution.py:20
  19.3 6.3 %collective-permute-start.3 = (bf16[12,6,1024]{2,1,0:T(8,128)(2,1)S(1)}, bf16[12,6,1024]{2,1,0:T(8,128)(2,1)S(1)}, u32[]{:S(2)}, u32[]{:S(2)}) collective-permute-start(bf16[12,6,1024]{2,1,0:T(8,128)(2,1)S(1)} %get-tuple-element.23), channel_id=1, source_target_pairs={{1,0},{2,1},{3,2},{4,3},{5,4},{6,5},{7,6},{0,7},{9,8},{10,9},{11,1... | collective-permute-start | bytes 442376 | tf_op jit(solution)/shard_map/ppermute | solution.py:21
  27.9 4.5 %copy-start.4 = (f32[1024]{0:T(1024)S(1)}, f32[1024]{0:T(1024)}, u32[]{:S(2)}) copy-start(f32[1024]{0:T(1024)} %param.12) | copy-start | bytes 12292
  38.0 3.2 %copy-start.2 = (f32[432,1024]{1,0:T(8,128)S(1)}, f32[432,1024]{1,0:T(8,128)}, u32[]{:S(2)}) copy-start(f32[432,1024]{1,0:T(8,128)} %reshape.102) | copy-start | bytes 5308420
  69.5 1.8 copy-start.3
  82.5 4.2 %copy-start.8 = (s32[4]{0:T(128)S(1)}, s32[4]{0:T(128)}, u32[]{:S(2)}) copy-start(s32[4]{0:T(128)} %param.19) | copy-start | bytes 52
  82.5 4.2 %copy-start.9 = (s32[1,8]{1,0:T(1,128)S(1)}, s32[1,8]{1,0:T(1,128)}, u32[]{:S(2)}) copy-start(s32[1,8]{1,0:T(1,128)} %param.20) | copy-start | bytes 100
  82.5 4.3 %copy-start.10 = (s32[5]{0:T(128)S(1)}, s32[5]{0:T(128)}, u32[]{:S(2)}) copy-start(s32[5]{0:T(128)} %param.21) | copy-start | bytes 64
  85.9 82.6 %all-gather.5.cloned.1.call-start = ((), (), s32[]{:S(2)}) async-start(), calls=%async_computation.3 | async-start | bytes 4177920 | tf_op jit(solution)/shard_map/all_gather | solution.py:133
  86.6 135.5 %reduce-scatter.7.cloned.1.call-start = ((), (), s32[]{:S(2)}) async-start(), calls=%async_computation.5 | async-start | bytes 2654208
  87.1 81.5 %copy-start.6 = (f32[5,1024]{1,0:T(8,128)S(1)}, f32[5,1024]{1,0:T(8,128)}, u32[]{:S(2)}) copy-start(f32[5,1024]{1,0:T(8,128)} %param.15) | copy-start | bytes 61444
  87.1 81.5 %copy-start.7 = (f32[5,1024]{1,0:T(8,128)S(1)}, f32[5,1024]{1,0:T(8,128)}, u32[]{:S(2)}) copy-start(f32[5,1024]{1,0:T(8,128)} %param.16) | copy-start | bytes 61444
  168.5 10.6 %copy-start.5 = (bf16[5,1024,320]{2,1,0:T(8,128)(2,1)S(1)}, bf16[5,1024,320]{2,1,0:T(8,128)(2,1)}, u32[]{:S(2)}) copy-start(bf16[5,1024,320]{2,1,0:T(8,128)(2,1)} %all-gather.5.cloned.1.call-done) | copy-start | bytes 9830404
  179.2 7.2 %copy-start.11 = (bf16[5,6,192,320]{3,2,1,0:T(8,128)(2,1)}, bf16[5,6,192,320]{3,2,1,0:T(8,128)(2,1)S(1)}, u32[]{:S(2)}) copy-start(bf16[5,6,192,320]{3,2,1,0:T(8,128)(2,1)S(1)} %multiply_convert_fusion) | copy-start | bytes 11059204
  188.1 117.2 %reduce-scatter.5.cloned.1.call-start = ((), (), s32[]{:S(2)}) async-start(), calls=%async_computation.4 | async-start | bytes 6684672 | tf_op jit(solution)/shard_map/reduce_scatter | solution.py:150
  205.7 101.6 %copy-start.1 = (bf16[1024,1024]{1,0:T(8,128)(2,1)S(1)}, bf16[1024,1024]{1,0:T(8,128)(2,1)}, u32[]{:S(2)}) copy-start(bf16[1024,1024]{1,0:T(8,128)(2,1)} %param.14) | copy-start | bytes 6291460
Sparse Core Ops, SparseCore 0:
  86.0 29.4 all-gather.2
  117.7 50.7 all-gather.4
  188.2 33.9 reduce-scatter.6
  225.5 79.7 reduce-scatter.4
where the time goes:
time: 315 us; the launch traced here: 314 us
  waiting for transfers between devices  183 us (58%)
  local copies, waits for them, and re-layouts  53.8 us (17%)
  matrix products  42.2 us (13%)
  between operations  14 us (4%)
  other arithmetic  12.5 us (4%)
  starting transfers between devices  7.98 us (3%)
    reduce_scatter x1, waiting for transfers between devices, local(): lax.psum_scatter(head_terms.astype(jnp.bfloat16), 'lat', scatter_dimensio...  80.9 us
    all_gather x1, waiting for transfers between devices, local(): heads_full = lax.all_gather(head_weight, 'lat', axis=1, tiled=True)  48.6 us
    all_gather x1, waiting for transfers between devices, local(): piece = lax.all_gather(latent, 'var', axis=1, tiled=True)  28.5 us
    unnamed x5, waiting for transfers between devices  17.3 us
    unnamed x32, local copies, waits for them, and re-layouts  13.9 us
    dot_general x1, matrix products, slot_terms(): jnp.einsum('krnd,kdo->krno', rows, heads_full, preferred_element_type=jnp...  10.6 us
    dot_general x1, matrix products, slot_terms(): jnp.einsum('krnd,krno->dko', rows, errors, preferred_element_type=jnp.flo...  9.29 us
    another operation x2, local copies, waits for them, and re-layouts, split(): shaped = values.reshape(win_rows, WH, win_cols, WW, parts, heads, head_size)  8.98 us
  transfers between devices with their start and end apart: 8, of which 7 were waited for; matrix products, arithmetic and copies ran while one was open for 8% of the time, Pallas kernels for 0%

commit v1 on v0

--- a/solution.py
+++ b/solution.py
@@ -132,7 +132,12 @@
     live_tiles = (slot_level[None, :] < tile_levels[:, None]).astype(jnp.float32)
     heads_full = lax.all_gather(head_weight, "lat", axis=1, tiled=True)
     tile_ids = jnp.arange(var_count, dtype=jnp.int32)
-    piece = lax.all_gather(latent, "var", axis=1, tiled=True)
+    ring = [latent]
+    for hop in range(7):
+        ring.append(lax.ppermute(ring[-1], "var", [(dev, (dev + 1) % 8) for dev in range(8)]))
+    piece = jnp.roll(
+        jnp.concatenate(ring[::-1], axis=1), (lax.axis_index("var") + 1) * ring[0].shape[1], axis=1
+    )
     piece_cols = piece.shape[1]
     column_tile = jnp.arange(piece_cols, dtype=jnp.int32) // band_cols
     onehot = (column_tile[:, None] == tile_ids[None, :]).astype(jnp.float32)

time: 315 us -> 287 us (0.911)
  waiting for transfers between devices: 183 us -> 156 us
    ppermute x0 -> x7, waiting for transfers between devices: none -> 50 us  [local(): lax.ppermute(ring[-1], 'var', [(dev, (dev + 1) % 8) for dev in range(8)])]
    all_gather x1, waiting for transfers between devices: 48.6 us -> 0.01 us  [local(): heads_full = lax.all_gather(head_weight, 'lat', axis=1, tiled=True)]
    all_gather x1 -> x0, waiting for transfers between devices: 28.5 us -> none  [local(): piece = lax.all_gather(latent, 'var', axis=1, tiled=True)]
    unnamed x32 -> x47, local copies, waits for them, and re-layouts: 13.9 us -> 14.2 us
    unnamed x5 -> x4, waiting for transfers between devices: 17.3 us -> 17.2 us
  transfers between devices with their start and end apart: 8 -> 14, of which waited for: 7 -> 12; matrix products, arithmetic and copies ran while one was open for 8% -> 30% of each run, Pallas kernels for 0% -> 0%
where the time goes in v1:
time: 287 us; the launch traced here: 286 us
  waiting for transfers between devices  156 us (54%)
  local copies, waits for them, and re-layouts  54.1 us (19%)
  matrix products  41.5 us (14%)
  between operations  14.1 us (5%)
  other arithmetic  11 us (4%)
  starting transfers between devices  9.21 us (3%)
    reduce_scatter x1, waiting for transfers between devices, local(): lax.psum_scatter(head_terms.astype(jnp.bfloat16), 'lat', scatter_dimensio...  81.1 us
    ppermute x7, waiting for transfers between devices, local(): lax.ppermute(ring[-1], 'var', [(dev, (dev + 1) % 8) for dev in range(8)])  50 us
    unnamed x4, waiting for transfers between devices  17.2 us
    unnamed x47, local copies, waits for them, and re-layouts  14.2 us
    dot_general x1, matrix products, slot_terms(): jnp.einsum('krnd,kdo->krno', rows, heads_full, preferred_element_type=jnp...  9.92 us
    dot_general x1, matrix products, slot_terms(): jnp.einsum('krnd,krno->dko', rows, errors, preferred_element_type=jnp.flo...  9.28 us
    another operation x2, local copies, waits for them, and re-layouts, split(): shaped = values.reshape(win_rows, WH, win_cols, WW, parts, heads, head_size)  8.97 us
    convert_element_type x1, local copies, waits for them, and re-layouts, local(): head_terms.astype(jnp.bfloat16)  8.2 us
  transfers between devices with their start and end apart: 14, of which 12 were waited for; matrix products, arithmetic and copies ran while one was open for 30% of the time, Pallas kernels for 0%

profile of v1, /device:TPU:0, one launch (start us, length us, event | category | flops | bytes accessed | tf_op | source)
XLA Modules:
  0.0 286.1 jit_solution(12468683539422280418)
XLA Ops:
  7.2 0.0 all-gather.2.cloned.1.call-start
  7.2 1.1 fusion.61
  8.4 3.6 %collective-permute-start = (bf16[3,24,1024]{2,1,0:T(8,128)(2,1)S(1)}, bf16[3,24,1024]{2,1,0:T(8,128)(2,1)S(1)}, u32[]{:S(2)}, u32[]{:S(2)}) collective-permute-start(bf16[3,24,1024]{2,1,0:T(8,128)(2,1)S(1)} %get-tuple-element.25), channel_id=1, source_target_pairs={{0,8},{8,16},{16,24},{24,32},{32,40},{40,48},{48,56},{56,64},{64,7... | collective-permute-start | bytes 442376 | tf_op jit(solution)/shard_map/ppermute | solution.py:20
  12.0 1.3 collective-permute-start.1
  13.3 1.8 collective-permute-done
  15.0 1.0 constant_dynamic-update-slice_fusion.1
  16.0 3.1 %collective-permute-done.1 = bf16[3,24,1024]{2,1,0:T(8,128)(2,1)S(1)} collective-permute-done((bf16[3,24,1024]{2,1,0:T(8,128)(2,1)S(1)}, bf16[3,24,1024]{2,1,0:T(8,128)(2,1)S(1)}, u32[]{:S(2)}, u32[]{:S(2)}) %collective-permute-start.1) | collective-permute-done | bytes 147488 | tf_op jit(solution)/shard_map/ppermute | solution.py:21
  19.2 0.1 fusion.60
  19.2 0.0 collective-permute-start.2
  19.3 2.9 %collective-permute-start.3 = (bf16[12,6,1024]{2,1,0:T(8,128)(2,1)S(1)}, bf16[12,6,1024]{2,1,0:T(8,128)(2,1)S(1)}, u32[]{:S(2)}, u32[]{:S(2)}) collective-permute-start(bf16[12,6,1024]{2,1,0:T(8,128)(2,1)S(1)} %get-tuple-element.23), channel_id=1, source_target_pairs={{1,0},{2,1},{3,2},{4,3},{5,4},{6,5},{7,6},{0,7},{9,8},{10,9},{11,1... | collective-permute-start | bytes 442376 | tf_op jit(solution)/shard_map/ppermute | solution.py:21
  22.2 0.0 all-gather.2.cloned.1.call-update
  22.2 0.0 reduce-scatter.7.cloned.1.call-start
  22.3 0.1 broadcast_in_dim.28
  22.4 0.1 broadcast_in_dim.29
  22.5 3.1 %collective-permute-done.2 = bf16[12,6,1024]{2,1,0:T(8,128)(2,1)S(1)} collective-permute-done((bf16[12,6,1024]{2,1,0:T(8,128)(2,1)S(1)}, bf16[12,6,1024]{2,1,0:T(8,128)(2,1)S(1)}, u32[]{:S(2)}, u32[]{:S(2)}) %collective-permute-start.2) | collective-permute-done | bytes 147488 | tf_op jit(solution)/shard_map/ppermute | solution.py:20
  25.6 0.4 fusion.58
  26.0 0.1 div.33
  26.1 1.8 multiply_reduce_fusion.1
  27.9 0.1 rsqrt.13
  28.0 0.1 slice.45
  28.1 1.6 maximum_convert_fusion
  29.7 2.6 reshape.102
  32.3 1.3 fusion.50
  33.6 2.2 fusion.40
  35.8 0.2 pad.4
  35.9 2.1 reshape.99
  38.1 3.1 %copy.48 = bf16[2,3,6,12,1,16,64]{6,5,3,2,1,0,4:T(8,128)(2,1)} copy(bf16[2,3,6,12,1,16,64]{6,5,3,1,2,0,4:T(8,128)(2,1)} %bitcast.58) | data formatting | bytes 1769472 | tf_op jit(solution)/shard_map/transpose | solution.py:42
  41.2 6.1 %fusion.15 = bf16[432,2048]{1,0:T(8,128)(2,1)} fusion(bf16[1024,3072]{1,0:T(8,128)(2,1)} %param.13, f32[432,1024]{1,0:T(8,128)} %reshape.102, f32[1024]{0:T(1024)S(1)} %copy-done.4, f32[432]{0:T(512)S(1)} %rsqrt.13, f32[432]{0:T(512)S(1)} %div.33), kind=kOutput, calls=%fused_computation.22 | convolution fusion | flops 1814593536 | bytes 7740800 | tf_op jit(solution)/shard_map/dot_general | solution.py:107
  47.3 6.4 %reshape_reshape.3 = bf16[2,6,3,12,2,16,64]{6,5,4,3,2,1,0:T(8,128)(2,1)} reshape(bf16[432,2048]{1,0:T(8,128)(2,1)} %fusion.15) | data formatting | bytes 3538944 | tf_op jit(solution)/shard_map/reshape;reshape | solution.py:41
  53.6 2.6 copy.46
  56.2 2.6 fusion.59
  58.8 4.0 %copy.61 = bf16[6,72,1,16,64]{1,4,3,0,2:T(8,128)(2,1)} copy(bf16[6,72,1,16,64]{4,3,2,1,0:T(8,128)(2,1)} %get-tuple-element.18) | data formatting | bytes 1769472
  62.9 4.1 %copy.62 = bf16[6,72,1,16,64]{1,4,3,0,2:T(8,128)(2,1)} copy(bf16[6,72,1,16,64]{4,3,2,1,0:T(8,128)(2,1)} %get-tuple-element.19) | data formatting | bytes 1769472
  66.9 3.1 %fusion.25 = f32[6,16,72,72]{2,3,1,0:T(8,128)S(1)} fusion(bf16[6,72,16,64]{3,2,1,0:T(8,128)(2,1)} %bitcast.59, bf16[6,72,1,16,64]{1,4,3,0,2:T(8,128)(2,1)} %copy.62), kind=kOutput, calls=%fused_computation.30 | convolution fusion | flops 63700992 | bytes 3760128 | tf_op jit(solution)/shard_map/wqhd,wkhd->whqk/dot_general | solution.py:53
  70.1 1.8 fusion.62
  71.9 1.9 fusion.34
  73.8 4.0 %copy.52 = bf16[6,72,16,64]{3,2,1,0:T(8,128)(2,1)} copy(bf16[6,72,16,64]{1,3,2,0:T(8,128)(2,1)} %fusion.34) | data formatting | bytes 1769472 | tf_op jit(solution)/shard_map/whqk,wkhd->wqhd/transpose | solution.py:60
  77.8 3.9 %reshape.100 = bf16[2,3,6,12,1024]{4,3,2,1,0:T(8,128)(2,1)} reshape(bf16[6,72,16,64]{3,2,1,0:T(8,128)(2,1)} %copy.52) | data formatting | bytes 1769472 | tf_op jit(solution)/shard_map/reshape | solution.py:62
  81.7 1.4 copy.53
  83.2 1.0 reshape.101
  84.2 1.6 fusion.43
  85.8 1.3 collective-permute-start.4
  87.1 6.2 %collective-permute-done.4 = bf16[6,24,1024]{2,1,0:T(8,128)(2,1)S(1)} collective-permute-done((bf16[6,24,1024]{2,1,0:T(8,128)(2,1)S(1)}, bf16[6,24,1024]{2,1,0:T(8,128)(2,1)S(1)}, u32[]{:S(2)}, u32[]{:S(2)}) %collective-permute-start.4) | collective-permute-done | bytes 294944 | tf_op jit(solution)/shard_map/ppermute | solution.py:137
  93.3 7.4 %collective-permute-done.5 = bf16[6,24,1024]{2,1,0:T(8,128)(2,1)S(1)} collective-permute-done((bf16[6,24,1024]{2,1,0:T(8,128)(2,1)S(1)}, bf16[6,24,1024]{2,1,0:T(8,128)(2,1)S(1)}, u32[]{:S(2)}, u32[]{:S(2)}) %collective-permute-start.5) | collective-permute-done | bytes 294944 | tf_op jit(solution)/shard_map/ppermute | solution.py:137
  100.6 7.4 %collective-permute-done.6 = bf16[6,24,1024]{2,1,0:T(8,128)(2,1)S(1)} collective-permute-done((bf16[6,24,1024]{2,1,0:T(8,128)(2,1)S(1)}, bf16[6,24,1024]{2,1,0:T(8,128)(2,1)S(1)}, u32[]{:S(2)}, u32[]{:S(2)}) %collective-permute-start.6) | collective-permute-done | bytes 294944 | tf_op jit(solution)/shard_map/ppermute | solution.py:137
  108.0 7.4 %collective-permute-done.7 = bf16[6,24,1024]{2,1,0:T(8,128)(2,1)S(1)} collective-permute-done((bf16[6,24,1024]{2,1,0:T(8,128)(2,1)S(1)}, bf16[6,24,1024]{2,1,0:T(8,128)(2,1)S(1)}, u32[]{:S(2)}, u32[]{:S(2)}) %collective-permute-start.7) | collective-permute-done | bytes 294944 | tf_op jit(solution)/shard_map/ppermute | solution.py:137
  115.4 7.4 %collective-permute-done.8 = bf16[6,24,1024]{2,1,0:T(8,128)(2,1)S(1)} collective-permute-done((bf16[6,24,1024]{2,1,0:T(8,128)(2,1)S(1)}, bf16[6,24,1024]{2,1,0:T(8,128)(2,1)S(1)}, u32[]{:S(2)}, u32[]{:S(2)}) %collective-permute-start.8) | collective-permute-done | bytes 294944 | tf_op jit(solution)/shard_map/ppermute | solution.py:137
  122.7 0.1 select_reduce_fusion
  122.8 7.3 %collective-permute-done.9 = bf16[6,24,1024]{2,1,0:T(8,128)(2,1)S(1)} collective-permute-done((bf16[6,24,1024]{2,1,0:T(8,128)(2,1)S(1)}, bf16[6,24,1024]{2,1,0:T(8,128)(2,1)S(1)}, u32[]{:S(2)}, u32[]{:S(2)}) %collective-permute-start.9) | collective-permute-done | bytes 294944 | tf_op jit(solution)/shard_map/ppermute | solution.py:137
  130.1 0.2 fusion.52
  130.3 7.1 %collective-permute-done.10 = bf16[6,24,1024]{2,1,0:T(8,128)(2,1)S(1)} collective-permute-done((bf16[6,24,1024]{2,1,0:T(8,128)(2,1)S(1)}, bf16[6,24,1024]{2,1,0:T(8,128)(2,1)S(1)}, u32[]{:S(2)}, u32[]{:S(2)}) %collective-permute-start.10) | collective-permute-done | bytes 294944 | tf_op jit(solution)/shard_map/ppermute | solution.py:137
  137.9 2.8 dynamic-slice_convert_fusion
  140.8 9.9 %multiply_convert_fusion = bf16[5,6,192,320]{3,2,1,0:T(8,128)(2,1)S(1)} fusion(bf16[5,6,192,320]{3,2,1,0:T(8,128)(2,1)} %param.18, f32[5,192]{1,0:T(8,128)S(1)} %fusion.52, bf16[5,1024,320]{2,1,0:T(8,128)(2,1)} %all-gather.2.cloned.1.call-done, f32[5,1024]{1,0:T(8,128)S(1)} %copy-done.7, f32[5,1024]{1,0:T(8,128)S(1)} %copy-done.6, ...), kind=kOutput, calls=%fused_computation.11 | convolution fusion | flops 3799941120 | bytes 15412992 | tf_op jit(solution)/shard_map/krnd,kdo->krno/dot_general | solution.py:73
  150.7 7.2 %multiply_reduce_fusion = bf16[6,192,1024]{2,1,0:T(8,128)(2,1)S(1)} fusion(f32[5,1024]{1,0:T(8,128)S(1)} %copy-done.6, bf16[5,6,192,320]{3,2,1,0:T(8,128)(2,1)S(1)} %multiply_convert_fusion, bf16[5,1024,320]{2,1,0:T(8,128)(2,1)S(1)} %copy-done.5), kind=kOutput, calls=%fused_computation.1 | convolution fusion | flops 3785490432 | bytes 9342976 | tf_op jit(solution)/shard_map/krno,kdo->krnd/dot_general | solution.py:77
  158.0 1.7 copy.63
  159.7 0.0 reduce-scatter.5.cloned.1.call-start
  159.7 9.3 %fusion.14 = bf16[1024,5,320]{0,2,1:T(8,128)(2,1)} fusion(bf16[5,6,192,320]{3,2,1,0:T(8,128)(2,1)} %copy-done.11, f32[5,1024]{1,0:T(8,128)S(1)} %copy-done.7, f32[5,1024]{1,0:T(8,128)S(1)} %copy-done.6, f32[6,192,1024]{2,1,0:T(8,128)} %dynamic-slice_convert_fusion), kind=kOutput, calls=%fused_computation.21 | convolution fusion | flops 3795845120 | bytes 11722752 | tf_op jit(solution)/shard_map/krnd,krno->dko/dot_general | solution.py:79
  169.0 8.2 %copy.54 = bf16[1024,5,320]{2,1,0:T(8,128)(2,1)} copy(bf16[1024,5,320]{0,2,1:T(8,128)(2,1)} %fusion.14) | data formatting | bytes 6553600 | tf_op jit(solution)/shard_map/convert_element_type | solution.py:156
  177.2 17.1 %reduce-scatter.7.cloned.1.call-done = bf16[24,6144]{1,0:T(8,128)(2,1)} async-done(((bf16[192,6144]{1,0:T(8,128)(2,1)}), bf16[24,6144]{1,0:T(8,128)(2,1)}) %reduce-scatter.7.cloned.1.call-update) | async-done | bytes 294928
  194.3 1.3 reshape.107
  195.7 0.9 copy.60
  196.6 81.1 %reduce-scatter.5.cloned.1.call-done = bf16[64,5,320]{2,1,0:T(8,128)(2,1)} async-done(((bf16[1024,5,320]{2,1,0:T(8,128)(2,1)}), bf16[64,5,320]{2,1,0:T(8,128)(2,1)}) %reduce-scatter.5.cloned.1.call-update) | async-done | bytes 204816 | tf_op jit(solution)/shard_map/reduce_scatter | solution.py:155
  277.7 1.0 convert_bitcast_fusion
  278.7 0.9 copy.55
  (56 shorter events, 0.5 us)
Async XLA Ops:
  7.2 77.0 %copy-start = (bf16[1024,1024]{1,0:T(8,128)(2,1)S(1)}, bf16[1024,1024]{1,0:T(8,128)(2,1)}, u32[]{:S(2)}) copy-start(bf16[1024,1024]{1,0:T(8,128)(2,1)} %param.14) | copy-start | bytes 6291460
  7.2 133.6 %all-gather.2.cloned.1.call-start = ((), (), s32[]{:S(2)}) async-start(), calls=%async_computation.2 | async-start | bytes 4177920 | tf_op jit(solution)/shard_map/all_gather | solution.py:133
  8.4 6.7 %collective-permute-start = (bf16[3,24,1024]{2,1,0:T(8,128)(2,1)S(1)}, bf16[3,24,1024]{2,1,0:T(8,128)(2,1)S(1)}, u32[]{:S(2)}, u32[]{:S(2)}) collective-permute-start(bf16[3,24,1024]{2,1,0:T(8,128)(2,1)S(1)} %get-tuple-element.25), channel_id=1, source_target_pairs={{0,8},{8,16},{16,24},{24,32},{32,40},{40,48},{48,56},{56,64},{64,7... | collective-permute-start | bytes 442376 | tf_op jit(solution)/shard_map/ppermute | solution.py:20
  12.0 7.2 %collective-permute-start.1 = (bf16[3,24,1024]{2,1,0:T(8,128)(2,1)S(1)}, bf16[3,24,1024]{2,1,0:T(8,128)(2,1)S(1)}, u32[]{:S(2)}, u32[]{:S(2)}) collective-permute-start(bf16[3,24,1024]{2,1,0:T(8,128)(2,1)S(1)} %get-tuple-element.24), channel_id=1, source_target_pairs={{8,0},{16,8},{24,16},{32,24},{40,32},{48,40},{56,48},{64,56},{72,6... | collective-permute-start | bytes 442376 | tf_op jit(solution)/shard_map/ppermute | solution.py:21
  19.2 6.3 %collective-permute-start.2 = (bf16[12,6,1024]{2,1,0:T(8,128)(2,1)S(1)}, bf16[12,6,1024]{2,1,0:T(8,128)(2,1)S(1)}, u32[]{:S(2)}, u32[]{:S(2)}) collective-permute-start(bf16[12,6,1024]{2,1,0:T(8,128)(2,1)S(1)} %get-tuple-element.22), channel_id=1, source_target_pairs={{0,1},{1,2},{2,3},{3,4},{4,5},{5,6},{6,7},{7,0},{8,9},{9,10},{10,1... | collective-permute-start | bytes 442376 | tf_op jit(solution)/shard_map/ppermute | solution.py:20
  19.3 6.3 %collective-permute-start.3 = (bf16[12,6,1024]{2,1,0:T(8,128)(2,1)S(1)}, bf16[12,6,1024]{2,1,0:T(8,128)(2,1)S(1)}, u32[]{:S(2)}, u32[]{:S(2)}) collective-permute-start(bf16[12,6,1024]{2,1,0:T(8,128)(2,1)S(1)} %get-tuple-element.23), channel_id=1, source_target_pairs={{1,0},{2,1},{3,2},{4,3},{5,4},{6,5},{7,6},{0,7},{9,8},{10,9},{11,1... | collective-permute-start | bytes 442376 | tf_op jit(solution)/shard_map/ppermute | solution.py:21
  22.2 172.1 %reduce-scatter.7.cloned.1.call-start = ((), (), s32[]{:S(2)}) async-start(), calls=%async_computation.4 | async-start | bytes 2654208
  27.9 4.4 %copy-start.4 = (f32[1024]{0:T(1024)S(1)}, f32[1024]{0:T(1024)}, u32[]{:S(2)}) copy-start(f32[1024]{0:T(1024)} %param.12) | copy-start | bytes 12292
  70.1 1.8 copy-start.2
  81.7 41.0 %copy-start.8 = (s32[4]{0:T(128)S(1)}, s32[4]{0:T(128)}, u32[]{:S(2)}) copy-start(s32[4]{0:T(128)} %param.19) | copy-start | bytes 52
  81.7 41.0 %copy-start.9 = (s32[1,8]{1,0:T(1,128)S(1)}, s32[1,8]{1,0:T(1,128)}, u32[]{:S(2)}) copy-start(s32[1,8]{1,0:T(1,128)} %param.20) | copy-start | bytes 100
  81.7 48.3 %copy-start.10 = (s32[5]{0:T(128)S(1)}, s32[5]{0:T(128)}, u32[]{:S(2)}) copy-start(s32[5]{0:T(128)} %param.21) | copy-start | bytes 64
  85.8 52.1 %copy-start.3 = (bf16[6,24,1024]{2,1,0:T(8,128)(2,1)}, bf16[6,24,1024]{2,1,0:T(8,128)(2,1)S(1)}, u32[]{:S(2)}) copy-start(bf16[6,24,1024]{2,1,0:T(8,128)(2,1)S(1)} %fusion.43) | copy-start | bytes 884740
  85.8 7.5 %collective-permute-start.4 = (bf16[6,24,1024]{2,1,0:T(8,128)(2,1)S(1)}, bf16[6,24,1024]{2,1,0:T(8,128)(2,1)S(1)}, u32[]{:S(2)}, u32[]{:S(2)}) collective-permute-start(bf16[6,24,1024]{2,1,0:T(8,128)(2,1)S(1)} %fusion.43), channel_id=1, source_target_pairs={{0,1},{1,2},{2,3},{3,4},{4,5},{5,6},{6,7},{7,0},{8,9},{9,10},{10,1... | collective-permute-start | bytes 884744 | tf_op jit(solution)/shard_map/ppermute | solution.py:137
  93.3 7.4 %collective-permute-start.5 = (bf16[6,24,1024]{2,1,0:T(8,128)(2,1)S(1)}, bf16[6,24,1024]{2,1,0:T(8,128)(2,1)S(1)}, u32[]{:S(2)}, u32[]{:S(2)}) collective-permute-start(bf16[6,24,1024]{2,1,0:T(8,128)(2,1)S(1)} %collective-permute-done.4), channel_id=1, source_target_pairs={{0,1},{1,2},{2,3},{3,4},{4,5},{5,6},{6,7},{7,0},{8,9},{9,10},{10,1... | collective-permute-start | bytes 884744 | tf_op jit(solution)/shard_map/ppermute | solution.py:137
  100.6 7.4 %collective-permute-start.6 = (bf16[6,24,1024]{2,1,0:T(8,128)(2,1)S(1)}, bf16[6,24,1024]{2,1,0:T(8,128)(2,1)S(1)}, u32[]{:S(2)}, u32[]{:S(2)}) collective-permute-start(bf16[6,24,1024]{2,1,0:T(8,128)(2,1)S(1)} %collective-permute-done.5), channel_id=1, source_target_pairs={{0,1},{1,2},{2,3},{3,4},{4,5},{5,6},{6,7},{7,0},{8,9},{9,10},{10,1... | collective-permute-start | bytes 884744 | tf_op jit(solution)/shard_map/ppermute | solution.py:137
  108.0 7.4 %collective-permute-start.7 = (bf16[6,24,1024]{2,1,0:T(8,128)(2,1)S(1)}, bf16[6,24,1024]{2,1,0:T(8,128)(2,1)S(1)}, u32[]{:S(2)}, u32[]{:S(2)}) collective-permute-start(bf16[6,24,1024]{2,1,0:T(8,128)(2,1)S(1)} %collective-permute-done.6), channel_id=1, source_target_pairs={{0,1},{1,2},{2,3},{3,4},{4,5},{5,6},{6,7},{7,0},{8,9},{9,10},{10,1... | collective-permute-start | bytes 884744 | tf_op jit(solution)/shard_map/ppermute | solution.py:137
  115.4 7.4 %collective-permute-start.8 = (bf16[6,24,1024]{2,1,0:T(8,128)(2,1)S(1)}, bf16[6,24,1024]{2,1,0:T(8,128)(2,1)S(1)}, u32[]{:S(2)}, u32[]{:S(2)}) collective-permute-start(bf16[6,24,1024]{2,1,0:T(8,128)(2,1)S(1)} %collective-permute-done.7), channel_id=1, source_target_pairs={{0,1},{1,2},{2,3},{3,4},{4,5},{5,6},{6,7},{7,0},{8,9},{9,10},{10,1... | collective-permute-start | bytes 884744 | tf_op jit(solution)/shard_map/ppermute | solution.py:137
  122.7 7.4 %collective-permute-start.9 = (bf16[6,24,1024]{2,1,0:T(8,128)(2,1)S(1)}, bf16[6,24,1024]{2,1,0:T(8,128)(2,1)S(1)}, u32[]{:S(2)}, u32[]{:S(2)}) collective-permute-start(bf16[6,24,1024]{2,1,0:T(8,128)(2,1)S(1)} %collective-permute-done.8), channel_id=1, source_target_pairs={{0,1},{1,2},{2,3},{3,4},{4,5},{5,6},{6,7},{7,0},{8,9},{9,10},{10,1... | collective-permute-start | bytes 884744 | tf_op jit(solution)/shard_map/ppermute | solution.py:137
  130.1 7.4 %collective-permute-start.10 = (bf16[6,24,1024]{2,1,0:T(8,128)(2,1)S(1)}, bf16[6,24,1024]{2,1,0:T(8,128)(2,1)S(1)}, u32[]{:S(2)}, u32[]{:S(2)}) collective-permute-start(bf16[6,24,1024]{2,1,0:T(8,128)(2,1)S(1)} %collective-permute-done.9), channel_id=1, source_target_pairs={{0,1},{1,2},{2,3},{3,4},{4,5},{5,6},{6,7},{7,0},{8,9},{9,10},{10,1... | collective-permute-start | bytes 884744 | tf_op jit(solution)/shard_map/ppermute | solution.py:137
  137.9 2.9 %copy-start.6 = (f32[5,1024]{1,0:T(8,128)S(1)}, f32[5,1024]{1,0:T(8,128)}, u32[]{:S(2)}) copy-start(f32[5,1024]{1,0:T(8,128)} %param.15) | copy-start | bytes 61444
  137.9 2.9 %copy-start.7 = (f32[5,1024]{1,0:T(8,128)S(1)}, f32[5,1024]{1,0:T(8,128)}, u32[]{:S(2)}) copy-start(f32[5,1024]{1,0:T(8,128)} %param.16) | copy-start | bytes 61444
  140.8 9.9 %copy-start.5 = (bf16[5,1024,320]{2,1,0:T(8,128)(2,1)S(1)}, bf16[5,1024,320]{2,1,0:T(8,128)(2,1)}, u32[]{:S(2)}) copy-start(bf16[5,1024,320]{2,1,0:T(8,128)(2,1)} %all-gather.2.cloned.1.call-done) | copy-start | bytes 9830404
  150.7 7.2 %copy-start.11 = (bf16[5,6,192,320]{3,2,1,0:T(8,128)(2,1)}, bf16[5,6,192,320]{3,2,1,0:T(8,128)(2,1)S(1)}, u32[]{:S(2)}) copy-start(bf16[5,6,192,320]{3,2,1,0:T(8,128)(2,1)S(1)} %multiply_convert_fusion) | copy-start | bytes 11059204
  159.7 118.0 %reduce-scatter.5.cloned.1.call-start = ((), (), s32[]{:S(2)}) async-start(), calls=%async_computation.3 | async-start | bytes 6684672 | tf_op jit(solution)/shard_map/reduce_scatter | solution.py:155
  177.2 102.4 %copy-start.1 = (bf16[1024,1024]{1,0:T(8,128)(2,1)S(1)}, bf16[1024,1024]{1,0:T(8,128)(2,1)}, u32[]{:S(2)}) copy-start(bf16[1024,1024]{1,0:T(8,128)(2,1)} %param.14) | copy-start | bytes 6291460
Sparse Core Ops, SparseCore 0:
  22.3 52.7 all-gather.1
  159.8 34.4 reduce-scatter.6
  197.8 79.8 reduce-scatter.4
